TPU v7x, 32 devices: a whole 2x2x4 slice. The times are simulated.
32 devices in a mesh: view: 2 (over core), gz: 8 (over z, y), gy: 2 (over x).
Axes of the slice: x: 2, y: 2, z: 4, core: 2. Of those that a mesh axis runs over, the one named last changes fastest.
Arguments:
- observed: float32 [2, 512, 32, 256], P('view', 'gz', 'gy'), may hold values from 0.5 to 4
- start: float32 [512, 32, 256], P('gz', 'gy'), may hold values from 0.5 to 2
- spread_z: float32 [2, 31], P('view'), may hold values from 0.05 to 1
- spread_y: float32 [2, 7], P('view'), may hold values from 0.1 to 1
- spread_x: float32 [2, 7], P('view'), may hold values from 0.1 to 1
Outputs:
- estimate: float32 [512, 32, 256], P('gz', 'gy')
All inputs are finite; a program needn't handle non-finite values.
Results may differ from a plain program's by a relative error of at most 0.0001.
Values sent between devices are 32-bit elements; how exact they have to be, the bound alone decides.
A program may use at most 64 MiB of HBM per device.

v0:
```python
import jax
import jax.numpy as jnp
from jax import lax
from jax.sharding import PartitionSpec as P

KZ = 31
KY = 7
KX = 7
ITERS = 2


def padded_2(x, sides, width):
    for axis, dim in sides:
        peers, length = (lax.axis_size(axis), x.shape[dim])
        up = [(i, (i + 1) % peers) for i in range(peers - 1)]
        down = [(j, i) for i, j in up]
        last = lax.slice_in_dim(x, length - width, length, axis=dim)
        first = lax.slice_in_dim(x, 0, width, axis=dim)
        before = lax.ppermute(last, axis, up)
        after = lax.ppermute(first, axis, down)
        x = jnp.concatenate([before, x, after], axis=dim)
    return x


def correlate(field, weights, along, margin):
    padding = [(0, 0), (0, 0), (0, 0)]
    padding[along] = (margin, margin)
    padded = jnp.pad(field, padding)
    taps = weights.shape[0]
    length = padded.shape[along] - taps + 1
    total = weights[0] * lax.slice_in_dim(padded, 0, length, 1, along)
    for offset in range(1, taps):
        total = total + weights[offset] * lax.slice_in_dim(
            padded, offset, offset + length, 1, along
        )
    return total


def blur_local(field, weight_z, weight_y, weight_x):
    padded = padded_2(field, (("gz", 0),), KZ // 2)
    field = correlate(padded, weight_z, 0, 0)
    padded = padded_2(field, (("gy", 1),), KY // 2)
    field = correlate(padded, weight_y, 1, 0)
    return correlate(field, weight_x, 2, KX // 2)


def on_device(observed, start, spread_z, spread_y, spread_x):
    recorded = observed[0]
    weight_z = spread_z[0] / jnp.sum(spread_z[0])
    weight_y = spread_y[0] / jnp.sum(spread_y[0])
    weight_x = spread_x[0] / jnp.sum(spread_x[0])
    estimate = start
    for sweep in range(ITERS):
        blurred = blur_local(estimate, weight_z, weight_y, weight_x)
        quotient = recorded / blurred
        correction = blur_local(quotient, weight_z[::-1], weight_y[::-1], weight_x[::-1])
        summed = lax.psum(correction, "view")
        estimate = estimate * (0.5 * summed)
    return estimate


def solution(mesh):
    return jax.shard_map(
        on_device,
        mesh=mesh,
        in_specs=(
            P("view", "gz", "gy", None),
            P("gz", "gy", None),
            P("view", None),
            P("view", None),
            P("view", None),
        ),
        out_specs=P("gz", "gy", None),
        check_vma=False,
    )
```

profile of v0, /device:TPU:0, one launch (start us, length us, event | category | flops | bytes accessed | tf_op | source)
XLA Modules:
  0.0 312.1 jit_solution(4010163259082128187)
XLA Ops:
  7.7 4.9 %collective-permute-start = (f32[15,16,256]{2,1,0:T(8,128)S(1)}, f32[15,16,256]{2,1,0:T(8,128)S(1)}, u32[]{:S(2)}, u32[]{:S(2)}) collective-permute-start(f32[15,16,256]{2,1,0:T(8,128)S(1)} %get-tuple-element.21), channel_id=1, source_target_pairs={{0,2},{2,4},{4,6},{6,8},{8,10},{10,12},{12,14},{1,3},{3,5},{5,7},{... | collective-permute-start | bytes 737288 | tf_op jit(solution)/shard_map/ppermute | solution.py:19
  12.6 1.3 collective-permute-start.1
  13.9 1.3 reduce_sum.29
  16.0 1.3 broadcast_divide_fusion
  18.0 1.3 reduce_sum.28
  20.0 1.3 broadcast_divide_fusion.2
  22.0 1.3 reduce_sum.27
  24.0 1.3 broadcast_divide_fusion.4
  25.7 23.5 %fusion.378 = f32[64,16,256]{2,1,0:T(8,128)S(1)} fusion(f32[79,16,256]{2,1,0:T(8,128)S(1)} %constant_dynamic-update-slice_fusion.2, f32[79,16,256]{2,1,0:T(8,128)S(1)} %get-tuple-element.19, f32[64,16,256]{2,1,0:T(8,128)S(1)} %copy-done, f32[]{:T(128)} %bitcast.39, f32[]{:T(128)} %bitcast.38, f32[]{:T(128)} %bitcast.37, f32[]{:T(128)} %bitcast.36, ...), kind=kLoop, calls=%fused_computation.617 | loop fusion | flops 15990784 | bytes 33554556 | tf_op jit(solution)/shard_map/add | solution.py:33
  49.3 1.3 collective-permute-start.3
  50.6 4.6 %collective-permute-start.2 = (f32[64,3,256]{2,1,0:T(4,128)S(1)}, f32[64,3,256]{2,1,0:T(4,128)S(1)}, u32[]{:S(2)}, u32[]{:S(2)}) collective-permute-start(f32[64,3,256]{2,1,0:T(4,128)S(1)} %get-tuple-element.17), channel_id=1, source_target_pairs={{0,1},{2,3},{4,5},{6,7},{8,9},{10,11},{12,13},{14,15},{16,17},{18,... | collective-permute-start | bytes 589832 | tf_op jit(solution)/shard_map/ppermute | solution.py:19
  56.5 2.4 collective-permute-done.3
  59.0 1.2 collective-permute-done.2
  60.2 5.4 %fusion.45 = f32[64,16,256]{2,1,0:T(8,128)S(1)} fusion(f32[64,16,256]{2,1,0:T(8,128)S(1)} %fusion.378, f32[64,3,256]{2,1,0:T(4,128)S(1)} %collective-permute-done.3, f32[64,3,256]{2,1,0:T(4,128)S(1)} %collective-permute-done.2, f32[]{:T(128)} %bitcast.45, f32[]{:T(128)} %bitcast.44, f32[]{:T(128)} %bitcast.43, f32[]{:T(128)} %bitcast.42, f32[]{:T(128)} %bitcast.41, ...), kind=kLoop, calls=%fused_computation.269 | loop fusion | flops 4980736 | bytes 2490396 | tf_op jit(solution)/shard_map/add | solution.py:33
  65.6 6.1 %fusion.321 = f32[64,16,256]{2,1,0:T(8,128)S(1)} fusion(f32[64,16,256]{2,1,0:T(8,128)S(1)} %fusion.45, f32[1,64,16,256]{3,2,1,0:T(8,128)S(1)} %copy-done.1, f32[]{:T(128)} %bitcast.51, f32[]{:T(128)} %bitcast.50, f32[]{:T(128)} %bitcast.49, f32[]{:T(128)} %bitcast.48, f32[]{:T(128)} %bitcast.47, f32[]{:T(128)} %bitcast.46, f32[]{:T(128)} %bitcast.7), kind=kLoop, calls=%fused_computation.545 | loop fusion | flops 3670016 | bytes 3145756 | tf_op jit(solution)/shard_map/div | solution.py:55
  71.7 1.3 collective-permute-start.5
  73.0 4.9 %collective-permute-start.4 = (f32[15,16,256]{2,1,0:T(8,128)S(1)}, f32[15,16,256]{2,1,0:T(8,128)S(1)}, u32[]{:S(2)}, u32[]{:S(2)}) collective-permute-start(f32[15,16,256]{2,1,0:T(8,128)S(1)} %get-tuple-element.15), channel_id=1, source_target_pairs={{0,2},{2,4},{4,6},{6,8},{8,10},{10,12},{12,14},{1,3},{3,5},{5,7},{... | collective-permute-start | bytes 737288 | tf_op jit(solution)/shard_map/ppermute | solution.py:19
  80.3 5.4 %collective-permute-done.4 = f32[15,16,256]{2,1,0:T(8,128)S(1)} collective-permute-done((f32[15,16,256]{2,1,0:T(8,128)S(1)}, f32[15,16,256]{2,1,0:T(8,128)S(1)}, u32[]{:S(2)}, u32[]{:S(2)}) %collective-permute-start.4) | collective-permute-done | bytes 245792 | tf_op jit(solution)/shard_map/ppermute | solution.py:19
  85.7 23.9 %fusion.231 = f32[64,16,256]{2,1,0:T(8,128)S(1)} fusion(f32[64,16,256]{2,1,0:T(8,128)S(1)} %fusion.321, f32[15,16,256]{2,1,0:T(8,128)S(1)} %collective-permute-done.5, f32[15,16,256]{2,1,0:T(8,128)S(1)} %collective-permute-done.4, f32[]{:T(128)} %bitcast.81, f32[]{:T(128)} %bitcast.80, f32[]{:T(128)} %bitcast.79, f32[]{:T(128)} %bitcast.78, f32[]{:T(128)} %bitcast.77, ...), kind=kLoop, calls=%fused_computation.455 | loop fusion | flops 23855104 | bytes 2588796 | tf_op jit(solution)/shard_map/add | solution.py:33
  109.7 1.3 collective-permute-start.7
  111.0 4.6 %collective-permute-start.6 = (f32[64,3,256]{2,1,0:T(4,128)S(1)}, f32[64,3,256]{2,1,0:T(4,128)S(1)}, u32[]{:S(2)}, u32[]{:S(2)}) collective-permute-start(f32[64,3,256]{2,1,0:T(4,128)S(1)} %get-tuple-element.13), channel_id=1, source_target_pairs={{0,1},{2,3},{4,5},{6,7},{8,9},{10,11},{12,13},{14,15},{16,17},{18,... | collective-permute-start | bytes 589832 | tf_op jit(solution)/shard_map/ppermute | solution.py:19
  116.9 2.9 collective-permute-done.7
  121.0 5.4 %fusion.31 = f32[64,16,256]{2,1,0:T(8,128)S(1)} fusion(f32[64,16,256]{2,1,0:T(8,128)S(1)} %fusion.231, f32[64,3,256]{2,1,0:T(4,128)S(1)} %collective-permute-done.7, f32[64,3,256]{2,1,0:T(4,128)S(1)} %collective-permute-done.6, f32[]{:T(128)} %bitcast.87, f32[]{:T(128)} %bitcast.86, f32[]{:T(128)} %bitcast.85, f32[]{:T(128)} %bitcast.84, f32[]{:T(128)} %bitcast.83, ...), kind=kLoop, calls=%fused_computation.255 | loop fusion | flops 4980736 | bytes 2490396 | tf_op jit(solution)/shard_map/add | solution.py:33
  126.5 6.8 %fusion.333 = f32[64,16,256]{2,1,0:T(8,128)} fusion(f32[64,16,256]{2,1,0:T(8,128)S(1)} %fusion.31, f32[]{:T(128)} %bitcast.93, f32[]{:T(128)} %bitcast.92, f32[]{:T(128)} %bitcast.91, f32[]{:T(128)} %bitcast.90, f32[]{:T(128)} %bitcast.89, f32[]{:T(128)} %bitcast.88, f32[]{:T(128)} %bitcast.1), kind=kLoop, calls=%fused_computation.557 | loop fusion | flops 3407872 | bytes 2097180 | tf_op jit(solution)/shard_map/add | solution.py:33
  133.4 21.7 %all-reduce.7.cloned.1.call-done = f32[64,16,256]{2,1,0:T(8,128)} async-done(((f32[64,16,256]{2,1,0:T(8,128)}), f32[64,16,256]{2,1,0:T(8,128)}) %all-reduce.7.cloned.1.call-update) | async-done | bytes 1048592 | tf_op jit(solution)/shard_map/psum | solution.py:57
  155.1 1.4 multiply_multiply_fusion.1
  156.6 1.3 collective-permute-start.9
  157.9 4.7 %collective-permute-start.8 = (f32[15,16,256]{2,1,0:T(8,128)S(1)}, f32[15,16,256]{2,1,0:T(8,128)S(1)}, u32[]{:S(2)}, u32[]{:S(2)}) collective-permute-start(f32[15,16,256]{2,1,0:T(8,128)S(1)} %get-tuple-element.11), channel_id=1, source_target_pairs={{0,2},{2,4},{4,6},{6,8},{8,10},{10,12},{12,14},{1,3},{3,5},{5,7},{... | collective-permute-start | bytes 737288 | tf_op jit(solution)/shard_map/ppermute | solution.py:19
  162.6 4.0 %collective-permute-done.9 = f32[15,16,256]{2,1,0:T(8,128)S(1)} collective-permute-done((f32[15,16,256]{2,1,0:T(8,128)S(1)}, f32[15,16,256]{2,1,0:T(8,128)S(1)}, u32[]{:S(2)}, u32[]{:S(2)}) %collective-permute-start.9) | collective-permute-done | bytes 245792 | tf_op jit(solution)/shard_map/ppermute | solution.py:20
  166.6 5.4 %collective-permute-done.8 = f32[15,16,256]{2,1,0:T(8,128)S(1)} collective-permute-done((f32[15,16,256]{2,1,0:T(8,128)S(1)}, f32[15,16,256]{2,1,0:T(8,128)S(1)}, u32[]{:S(2)}, u32[]{:S(2)}) %collective-permute-start.8) | collective-permute-done | bytes 245792 | tf_op jit(solution)/shard_map/ppermute | solution.py:19
  172.0 23.7 %fusion.145 = f32[64,16,256]{2,1,0:T(8,128)S(1)} fusion(f32[64,16,256]{2,1,0:T(8,128)S(1)} %multiply_multiply_fusion.1, f32[15,16,256]{2,1,0:T(8,128)S(1)} %collective-permute-done.9, f32[15,16,256]{2,1,0:T(8,128)S(1)} %collective-permute-done.8, f32[]{:T(128)} %bitcast.39, f32[]{:T(128)} %bitcast.38, f32[]{:T(128)} %bitcast.37, f32[]{:T(128)} %bitcast.36, ...), kind=kLoop, calls=%fused_computation.369 | loop fusion | flops 23855104 | bytes 2588796 | tf_op jit(solution)/shard_map/add | solution.py:33
  195.9 1.3 collective-permute-start.11
  197.2 4.6 %collective-permute-start.10 = (f32[64,3,256]{2,1,0:T(4,128)S(1)}, f32[64,3,256]{2,1,0:T(4,128)S(1)}, u32[]{:S(2)}, u32[]{:S(2)}) collective-permute-start(f32[64,3,256]{2,1,0:T(4,128)S(1)} %get-tuple-element.9), channel_id=1, source_target_pairs={{0,1},{2,3},{4,5},{6,7},{8,9},{10,11},{12,13},{14,15},{16,17},{18,... | collective-permute-start | bytes 589832 | tf_op jit(solution)/shard_map/ppermute | solution.py:19
  201.8 4.2 %collective-permute-done.11 = f32[64,3,256]{2,1,0:T(4,128)S(1)} collective-permute-done((f32[64,3,256]{2,1,0:T(4,128)S(1)}, f32[64,3,256]{2,1,0:T(4,128)S(1)}, u32[]{:S(2)}, u32[]{:S(2)}) %collective-permute-start.11) | collective-permute-done | bytes 196640 | tf_op jit(solution)/shard_map/ppermute | solution.py:20
  207.2 5.3 %fusion.17 = f32[64,16,256]{2,1,0:T(8,128)S(1)} fusion(f32[64,16,256]{2,1,0:T(8,128)S(1)} %fusion.145, f32[64,3,256]{2,1,0:T(4,128)S(1)} %collective-permute-done.11, f32[64,3,256]{2,1,0:T(4,128)S(1)} %collective-permute-done.10, f32[]{:T(128)} %bitcast.45, f32[]{:T(128)} %bitcast.44, f32[]{:T(128)} %bitcast.43, f32[]{:T(128)} %bitcast.42, f32[]{:T(128)} %bitcast.41, ...), kind=kLoop, calls=%fused_computation.241 | loop fusion | flops 4980736 | bytes 2490396 | tf_op jit(solution)/shard_map/add | solution.py:33
  212.5 6.1 %fusion.346 = f32[64,16,256]{2,1,0:T(8,128)S(1)} fusion(f32[64,16,256]{2,1,0:T(8,128)S(1)} %fusion.17, f32[1,64,16,256]{3,2,1,0:T(8,128)S(1)} %copy-done.1, f32[]{:T(128)} %bitcast.51, f32[]{:T(128)} %bitcast.50, f32[]{:T(128)} %bitcast.49, f32[]{:T(128)} %bitcast.48, f32[]{:T(128)} %bitcast.47, f32[]{:T(128)} %bitcast.46, f32[]{:T(128)} %bitcast.7), kind=kLoop, calls=%fused_computation.570 | loop fusion | flops 3670016 | bytes 3145756 | tf_op jit(solution)/shard_map/div | solution.py:55
  218.7 1.3 collective-permute-start.13
  220.0 5.0 %collective-permute-start.12 = (f32[15,16,256]{2,1,0:T(8,128)S(1)}, f32[15,16,256]{2,1,0:T(8,128)S(1)}, u32[]{:S(2)}, u32[]{:S(2)}) collective-permute-start(f32[15,16,256]{2,1,0:T(8,128)S(1)} %get-tuple-element.7), channel_id=1, source_target_pairs={{0,2},{2,4},{4,6},{6,8},{8,10},{10,12},{12,14},{1,3},{3,5},{5,7},{... | collective-permute-start | bytes 737288 | tf_op jit(solution)/shard_map/ppermute | solution.py:19
  225.0 3.1 collective-permute-done.13
  228.1 5.4 %collective-permute-done.12 = f32[15,16,256]{2,1,0:T(8,128)S(1)} collective-permute-done((f32[15,16,256]{2,1,0:T(8,128)S(1)}, f32[15,16,256]{2,1,0:T(8,128)S(1)}, u32[]{:S(2)}, u32[]{:S(2)}) %collective-permute-start.12) | collective-permute-done | bytes 245792 | tf_op jit(solution)/shard_map/ppermute | solution.py:19
  233.5 23.9 %fusion.59 = f32[64,16,256]{2,1,0:T(8,128)S(1)} fusion(f32[64,16,256]{2,1,0:T(8,128)S(1)} %fusion.346, f32[15,16,256]{2,1,0:T(8,128)S(1)} %collective-permute-done.13, f32[15,16,256]{2,1,0:T(8,128)S(1)} %collective-permute-done.12, f32[]{:T(128)} %bitcast.81, f32[]{:T(128)} %bitcast.80, f32[]{:T(128)} %bitcast.79, f32[]{:T(128)} %bitcast.78, f32[]{:T(128)} %bitcast.77, ...), kind=kLoop, calls=%fused_computation.283 | loop fusion | flops 23855104 | bytes 2588796 | tf_op jit(solution)/shard_map/add | solution.py:33
  257.5 1.3 collective-permute-start.15
  258.8 4.6 %collective-permute-start.14 = (f32[64,3,256]{2,1,0:T(4,128)S(1)}, f32[64,3,256]{2,1,0:T(4,128)S(1)}, u32[]{:S(2)}, u32[]{:S(2)}) collective-permute-start(f32[64,3,256]{2,1,0:T(4,128)S(1)} %get-tuple-element.5), channel_id=1, source_target_pairs={{0,1},{2,3},{4,5},{6,7},{8,9},{10,11},{12,13},{14,15},{16,17},{18,... | collective-permute-start | bytes 589832 | tf_op jit(solution)/shard_map/ppermute | solution.py:19
  263.4 4.4 %collective-permute-done.15 = f32[64,3,256]{2,1,0:T(4,128)S(1)} collective-permute-done((f32[64,3,256]{2,1,0:T(4,128)S(1)}, f32[64,3,256]{2,1,0:T(4,128)S(1)}, u32[]{:S(2)}, u32[]{:S(2)}) %collective-permute-start.15) | collective-permute-done | bytes 196640 | tf_op jit(solution)/shard_map/ppermute | solution.py:20
  268.9 5.4 %fusion.3 = f32[64,16,256]{2,1,0:T(8,128)S(1)} fusion(f32[64,16,256]{2,1,0:T(8,128)S(1)} %fusion.59, f32[64,3,256]{2,1,0:T(4,128)S(1)} %collective-permute-done.15, f32[64,3,256]{2,1,0:T(4,128)S(1)} %collective-permute-done.14, f32[]{:T(128)} %bitcast.87, f32[]{:T(128)} %bitcast.86, f32[]{:T(128)} %bitcast.85, f32[]{:T(128)} %bitcast.84, f32[]{:T(128)} %bitcast.83, ...), kind=kLoop, calls=%fused_computation.227 | loop fusion | flops 4980736 | bytes 2490396 | tf_op jit(solution)/shard_map/add | solution.py:33
  274.4 6.8 %fusion.358 = f32[64,16,256]{2,1,0:T(8,128)} fusion(f32[64,16,256]{2,1,0:T(8,128)S(1)} %fusion.3, f32[]{:T(128)} %bitcast.93, f32[]{:T(128)} %bitcast.92, f32[]{:T(128)} %bitcast.91, f32[]{:T(128)} %bitcast.90, f32[]{:T(128)} %bitcast.89, f32[]{:T(128)} %bitcast.88, f32[]{:T(128)} %bitcast.1), kind=kLoop, calls=%fused_computation.582 | loop fusion | flops 3407872 | bytes 2097180 | tf_op jit(solution)/shard_map/add | solution.py:33
  281.2 21.6 %all-reduce.9.cloned.1.call-done = f32[64,16,256]{2,1,0:T(8,128)} async-done(((f32[64,16,256]{2,1,0:T(8,128)}), f32[64,16,256]{2,1,0:T(8,128)}) %all-reduce.9.cloned.1.call-update) | async-done | bytes 1048592 | tf_op jit(solution)/shard_map/psum | solution.py:57
  302.8 2.4 multiply_multiply_fusion
  (36 shorter events, 14.2 us)
Async XLA Ops:
  6.5 18.8 %copy-start = (f32[64,16,256]{2,1,0:T(8,128)S(1)}, f32[64,16,256]{2,1,0:T(8,128)}, u32[]{:S(2)}) copy-start(f32[64,16,256]{2,1,0:T(8,128)} %param.6) | copy-start | bytes 3145732
  6.5 148.5 %all-reduce.7.cloned.1.call-start = ((), (), s32[]{:S(2)}) async-start(), calls=%async_computation | async-start | bytes 2097152 | tf_op jit(solution)/shard_map/psum | solution.py:57
  7.7 17.6 %collective-permute-start = (f32[15,16,256]{2,1,0:T(8,128)S(1)}, f32[15,16,256]{2,1,0:T(8,128)S(1)}, u32[]{:S(2)}, u32[]{:S(2)}) collective-permute-start(f32[15,16,256]{2,1,0:T(8,128)S(1)} %get-tuple-element.21), channel_id=1, source_target_pairs={{0,2},{2,4},{4,6},{6,8},{8,10},{10,12},{12,14},{1,3},{3,5},{5,7},{... | collective-permute-start | bytes 737288 | tf_op jit(solution)/shard_map/ppermute | solution.py:19
  12.6 13.0 %collective-permute-start.1 = (f32[15,16,256]{2,1,0:T(8,128)S(1)}, f32[15,16,256]{2,1,0:T(8,128)S(1)}, u32[]{:S(2)}, u32[]{:S(2)}) collective-permute-start(f32[15,16,256]{2,1,0:T(8,128)S(1)} %get-tuple-element.22), channel_id=1, source_target_pairs={{2,0},{4,2},{6,4},{8,6},{10,8},{12,10},{14,12},{3,1},{5,3},{7,5},{... | collective-permute-start | bytes 737288 | tf_op jit(solution)/shard_map/ppermute | solution.py:20
  49.3 9.7 %collective-permute-start.3 = (f32[64,3,256]{2,1,0:T(4,128)S(1)}, f32[64,3,256]{2,1,0:T(4,128)S(1)}, u32[]{:S(2)}, u32[]{:S(2)}) collective-permute-start(f32[64,3,256]{2,1,0:T(4,128)S(1)} %get-tuple-element.18), channel_id=1, source_target_pairs={{1,0},{3,2},{5,4},{7,6},{9,8},{11,10},{13,12},{15,14},{17,16},{19,... | collective-permute-start | bytes 589832 | tf_op jit(solution)/shard_map/ppermute | solution.py:20
  50.6 9.6 %collective-permute-start.2 = (f32[64,3,256]{2,1,0:T(4,128)S(1)}, f32[64,3,256]{2,1,0:T(4,128)S(1)}, u32[]{:S(2)}, u32[]{:S(2)}) collective-permute-start(f32[64,3,256]{2,1,0:T(4,128)S(1)} %get-tuple-element.17), channel_id=1, source_target_pairs={{0,1},{2,3},{4,5},{6,7},{8,9},{10,11},{12,13},{14,15},{16,17},{18,... | collective-permute-start | bytes 589832 | tf_op jit(solution)/shard_map/ppermute | solution.py:19
  60.2 5.4 %copy-start.1 = (f32[1,64,16,256]{3,2,1,0:T(8,128)S(1)}, f32[1,64,16,256]{3,2,1,0:T(8,128)}, u32[]{:S(2)}) copy-start(f32[1,64,16,256]{3,2,1,0:T(8,128)} %param.5) | copy-start | bytes 3145732
  71.7 8.5 %collective-permute-start.5 = (f32[15,16,256]{2,1,0:T(8,128)S(1)}, f32[15,16,256]{2,1,0:T(8,128)S(1)}, u32[]{:S(2)}, u32[]{:S(2)}) collective-permute-start(f32[15,16,256]{2,1,0:T(8,128)S(1)} %get-tuple-element.16), channel_id=1, source_target_pairs={{2,0},{4,2},{6,4},{8,6},{10,8},{12,10},{14,12},{3,1},{5,3},{7,5},{... | collective-permute-start | bytes 737288 | tf_op jit(solution)/shard_map/ppermute | solution.py:20
  73.0 12.6 %collective-permute-start.4 = (f32[15,16,256]{2,1,0:T(8,128)S(1)}, f32[15,16,256]{2,1,0:T(8,128)S(1)}, u32[]{:S(2)}, u32[]{:S(2)}) collective-permute-start(f32[15,16,256]{2,1,0:T(8,128)S(1)} %get-tuple-element.15), channel_id=1, source_target_pairs={{0,2},{2,4},{4,6},{6,8},{8,10},{10,12},{12,14},{1,3},{3,5},{5,7},{... | collective-permute-start | bytes 737288 | tf_op jit(solution)/shard_map/ppermute | solution.py:19
  109.7 10.1 %collective-permute-start.7 = (f32[64,3,256]{2,1,0:T(4,128)S(1)}, f32[64,3,256]{2,1,0:T(4,128)S(1)}, u32[]{:S(2)}, u32[]{:S(2)}) collective-permute-start(f32[64,3,256]{2,1,0:T(4,128)S(1)} %get-tuple-element.14), channel_id=1, source_target_pairs={{1,0},{3,2},{5,4},{7,6},{9,8},{11,10},{13,12},{15,14},{17,16},{19,... | collective-permute-start | bytes 589832 | tf_op jit(solution)/shard_map/ppermute | solution.py:20
  111.0 10.0 %collective-permute-start.6 = (f32[64,3,256]{2,1,0:T(4,128)S(1)}, f32[64,3,256]{2,1,0:T(4,128)S(1)}, u32[]{:S(2)}, u32[]{:S(2)}) collective-permute-start(f32[64,3,256]{2,1,0:T(4,128)S(1)} %get-tuple-element.13), channel_id=1, source_target_pairs={{0,1},{2,3},{4,5},{6,7},{8,9},{10,11},{12,13},{14,15},{16,17},{18,... | collective-permute-start | bytes 589832 | tf_op jit(solution)/shard_map/ppermute | solution.py:19
  133.3 169.5 %all-reduce.9.cloned.1.call-start = ((), (), s32[]{:S(2)}) async-start(), calls=%async_computation.1 | async-start | bytes 2097152 | tf_op jit(solution)/shard_map/psum | solution.py:57
  156.6 10.1 %collective-permute-start.9 = (f32[15,16,256]{2,1,0:T(8,128)S(1)}, f32[15,16,256]{2,1,0:T(8,128)S(1)}, u32[]{:S(2)}, u32[]{:S(2)}) collective-permute-start(f32[15,16,256]{2,1,0:T(8,128)S(1)} %get-tuple-element.12), channel_id=1, source_target_pairs={{2,0},{4,2},{6,4},{8,6},{10,8},{12,10},{14,12},{3,1},{5,3},{7,5},{... | collective-permute-start | bytes 737288 | tf_op jit(solution)/shard_map/ppermute | solution.py:20
  157.9 14.2 %collective-permute-start.8 = (f32[15,16,256]{2,1,0:T(8,128)S(1)}, f32[15,16,256]{2,1,0:T(8,128)S(1)}, u32[]{:S(2)}, u32[]{:S(2)}) collective-permute-start(f32[15,16,256]{2,1,0:T(8,128)S(1)} %get-tuple-element.11), channel_id=1, source_target_pairs={{0,2},{2,4},{4,6},{6,8},{8,10},{10,12},{12,14},{1,3},{3,5},{5,7},{... | collective-permute-start | bytes 737288 | tf_op jit(solution)/shard_map/ppermute | solution.py:19
  195.9 10.1 %collective-permute-start.11 = (f32[64,3,256]{2,1,0:T(4,128)S(1)}, f32[64,3,256]{2,1,0:T(4,128)S(1)}, u32[]{:S(2)}, u32[]{:S(2)}) collective-permute-start(f32[64,3,256]{2,1,0:T(4,128)S(1)} %get-tuple-element.10), channel_id=1, source_target_pairs={{1,0},{3,2},{5,4},{7,6},{9,8},{11,10},{13,12},{15,14},{17,16},{19,... | collective-permute-start | bytes 589832 | tf_op jit(solution)/shard_map/ppermute | solution.py:20
  197.2 10.0 %collective-permute-start.10 = (f32[64,3,256]{2,1,0:T(4,128)S(1)}, f32[64,3,256]{2,1,0:T(4,128)S(1)}, u32[]{:S(2)}, u32[]{:S(2)}) collective-permute-start(f32[64,3,256]{2,1,0:T(4,128)S(1)} %get-tuple-element.9), channel_id=1, source_target_pairs={{0,1},{2,3},{4,5},{6,7},{8,9},{10,11},{12,13},{14,15},{16,17},{18,... | collective-permute-start | bytes 589832 | tf_op jit(solution)/shard_map/ppermute | solution.py:19
  218.7 9.4 %collective-permute-start.13 = (f32[15,16,256]{2,1,0:T(8,128)S(1)}, f32[15,16,256]{2,1,0:T(8,128)S(1)}, u32[]{:S(2)}, u32[]{:S(2)}) collective-permute-start(f32[15,16,256]{2,1,0:T(8,128)S(1)} %get-tuple-element.8), channel_id=1, source_target_pairs={{2,0},{4,2},{6,4},{8,6},{10,8},{12,10},{14,12},{3,1},{5,3},{7,5},{... | collective-permute-start | bytes 737288 | tf_op jit(solution)/shard_map/ppermute | solution.py:20
  220.0 13.5 %collective-permute-start.12 = (f32[15,16,256]{2,1,0:T(8,128)S(1)}, f32[15,16,256]{2,1,0:T(8,128)S(1)}, u32[]{:S(2)}, u32[]{:S(2)}) collective-permute-start(f32[15,16,256]{2,1,0:T(8,128)S(1)} %get-tuple-element.7), channel_id=1, source_target_pairs={{0,2},{2,4},{4,6},{6,8},{8,10},{10,12},{12,14},{1,3},{3,5},{5,7},{... | collective-permute-start | bytes 737288 | tf_op jit(solution)/shard_map/ppermute | solution.py:19
  257.5 10.2 %collective-permute-start.15 = (f32[64,3,256]{2,1,0:T(4,128)S(1)}, f32[64,3,256]{2,1,0:T(4,128)S(1)}, u32[]{:S(2)}, u32[]{:S(2)}) collective-permute-start(f32[64,3,256]{2,1,0:T(4,128)S(1)} %get-tuple-element.6), channel_id=1, source_target_pairs={{1,0},{3,2},{5,4},{7,6},{9,8},{11,10},{13,12},{15,14},{17,16},{19,... | collective-permute-start | bytes 589832 | tf_op jit(solution)/shard_map/ppermute | solution.py:20
  258.8 10.1 %collective-permute-start.14 = (f32[64,3,256]{2,1,0:T(4,128)S(1)}, f32[64,3,256]{2,1,0:T(4,128)S(1)}, u32[]{:S(2)}, u32[]{:S(2)}) collective-permute-start(f32[64,3,256]{2,1,0:T(4,128)S(1)} %get-tuple-element.5), channel_id=1, source_target_pairs={{0,1},{2,3},{4,5},{6,7},{8,9},{10,11},{12,13},{14,15},{16,17},{18,... | collective-permute-start | bytes 589832 | tf_op jit(solution)/shard_map/ppermute | solution.py:19
Sparse Core Ops, SparseCore 0:
  133.4 21.5 all-reduce.6
  281.4 21.4 all-reduce.8
where the time goes:
time: 314 us; the launch traced here: 312 us
  other arithmetic  154 us (49%)
  waiting for transfers between devices  86.3 us (27%)
  starting transfers between devices  48.3 us (15%)
  between operations  13.7 us (4%)
  local copies, waits for them, and re-layouts  9.71 us (3%)
    add x10, other arithmetic, correlate(): total + weights[offset] * lax.slice_in_dim(padded, offset, offset + lengt...  130 us
    psum x2, waiting for transfers between devices, on_device(): summed = lax.psum(correction, 'view')  43.3 us
    ppermute x8, starting transfers between devices, padded_2(): before = lax.ppermute(last, axis, up)  37.9 us
    ppermute x8, waiting for transfers between devices, padded_2(): after = lax.ppermute(first, axis, down)  21.9 us
    ppermute x8, waiting for transfers between devices, padded_2(): before = lax.ppermute(last, axis, up)  21 us
    div x2, other arithmetic, on_device(): quotient = recorded / blurred  12.2 us
    ppermute x8, starting transfers between devices, padded_2(): after = lax.ppermute(first, axis, down)  10.3 us
  transfers between devices with their start and end apart: 18, of which 16 were waited for; matrix products, arithmetic and copies ran while one was open for 5% of the time, Pallas kernels for 0%

commit v1 on v0

--- a/solution.py
+++ b/solution.py
@@ -54,7 +54,7 @@
         blurred = blur_local(estimate, weight_z, weight_y, weight_x)
         quotient = recorded / blurred
         correction = blur_local(quotient, weight_z[::-1], weight_y[::-1], weight_x[::-1])
-        summed = lax.psum(correction, "view")
+        summed = jnp.sum(lax.all_gather(correction, "view"), axis=0)
         estimate = estimate * (0.5 * summed)
     return estimate
 

time: 314 us -> 299 us (0.952)
  starting transfers between devices: 48.3 us -> 37.8 us
  waiting for transfers between devices: 86.3 us -> 80.1 us
    psum x2 -> x0, waiting for transfers between devices: 43.3 us -> none  [on_device(): summed = lax.psum(correction, 'view')]
    all_gather x0 -> x2, waiting for transfers between devices: none -> 29.3 us  [on_device(): summed = jnp.sum(lax.all_gather(correction, 'view'), axis=0)]
    ppermute x8, starting transfers between devices: 37.9 us -> 27.1 us  [padded_2(): before = lax.ppermute(last, axis, up)]
    ppermute x8, waiting for transfers between devices: 21 us -> 25.5 us  [padded_2(): before = lax.ppermute(last, axis, up)]
    reduce_sum x0 -> x2, other arithmetic: none -> 3.78 us  [on_device(): summed = jnp.sum(lax.all_gather(correction, 'view'), axis=0)]
    ppermute x8, waiting for transfers between devices: 21.9 us -> 25.2 us  [padded_2(): after = lax.ppermute(first, axis, down)]
  transfers between devices with their start and end apart: 18 -> 18, of which waited for: 16 -> 15; matrix products, arithmetic and copies ran while one was open for 5% -> 5% of each run, Pallas kernels for 0% -> 0%
where the time goes in v1:
time: 299 us; the launch traced here: 297 us
  other arithmetic  155 us (52%)
  waiting for transfers between devices  80.1 us (27%)
  starting transfers between devices  37.8 us (13%)
  between operations  13.8 us (5%)
  local copies, waits for them, and re-layouts  9.74 us (3%)
    add x10, other arithmetic, correlate(): total + weights[offset] * lax.slice_in_dim(padded, offset, offset + lengt...  130 us
    all_gather x2, waiting for transfers between devices, on_device(): summed = jnp.sum(lax.all_gather(correction, 'view'), axis=0)  29.3 us
    ppermute x8, starting transfers between devices, padded_2(): before = lax.ppermute(last, axis, up)  27.1 us
    ppermute x8, waiting for transfers between devices, padded_2(): before = lax.ppermute(last, axis, up)  25.5 us
    ppermute x8, waiting for transfers between devices, padded_2(): after = lax.ppermute(first, axis, down)  25.2 us
    div x2, other arithmetic, on_device(): quotient = recorded / blurred  11.9 us
    ppermute x8, starting transfers between devices, padded_2(): after = lax.ppermute(first, axis, down)  10.5 us
  transfers between devices with their start and end apart: 18, of which 15 were waited for; matrix products, arithmetic and copies ran while one was open for 5% of the time, Pallas kernels for 0%

profile of v1, /device:TPU:0, one launch (start us, length us, event | category | flops | bytes accessed | tf_op | source)
XLA Modules:
  0.0 296.6 jit_solution(13065002100297404981)
XLA Ops:
  7.7 4.9 %collective-permute-start = (f32[15,16,256]{2,1,0:T(8,128)S(1)}, f32[15,16,256]{2,1,0:T(8,128)S(1)}, u32[]{:S(2)}, u32[]{:S(2)}) collective-permute-start(f32[15,16,256]{2,1,0:T(8,128)S(1)} %get-tuple-element.21), channel_id=1, source_target_pairs={{0,2},{2,4},{4,6},{6,8},{8,10},{10,12},{12,14},{1,3},{3,5},{5,7},{... | collective-permute-start | bytes 737288 | tf_op jit(solution)/shard_map/ppermute | solution.py:19
  12.6 1.3 collective-permute-start.1
  13.9 1.3 reduce_sum.45
  18.0 1.3 broadcast_divide_fusion
  20.0 1.3 broadcast_divide_fusion.4
  24.0 1.3 broadcast_divide_fusion.2
  25.7 23.5 %fusion.378 = f32[64,16,256]{2,1,0:T(8,128)S(1)} fusion(f32[79,16,256]{2,1,0:T(8,128)S(1)} %constant_dynamic-update-slice_fusion.2, f32[79,16,256]{2,1,0:T(8,128)S(1)} %get-tuple-element.19, f32[64,16,256]{2,1,0:T(8,128)S(1)} %copy-done, f32[]{:T(128)} %bitcast.39, f32[]{:T(128)} %bitcast.38, f32[]{:T(128)} %bitcast.37, f32[]{:T(128)} %bitcast.36, ...), kind=kLoop, calls=%fused_computation.617 | loop fusion | flops 15990784 | bytes 33554556 | tf_op jit(solution)/shard_map/add | solution.py:33
  49.3 3.4 %collective-permute-start.2 = (f32[64,3,256]{2,1,0:T(4,128)S(1)}, f32[64,3,256]{2,1,0:T(4,128)S(1)}, u32[]{:S(2)}, u32[]{:S(2)}) collective-permute-start(f32[64,3,256]{2,1,0:T(4,128)S(1)} %get-tuple-element.17), channel_id=1, source_target_pairs={{0,1},{2,3},{4,5},{6,7},{8,9},{10,11},{12,13},{14,15},{16,17},{18,... | collective-permute-start | bytes 589832 | tf_op jit(solution)/shard_map/ppermute | solution.py:19
  52.7 1.3 collective-permute-start.3
  55.3 2.6 collective-permute-done.2
  57.9 4.1 %collective-permute-done.3 = f32[64,3,256]{2,1,0:T(4,128)S(1)} collective-permute-done((f32[64,3,256]{2,1,0:T(4,128)S(1)}, f32[64,3,256]{2,1,0:T(4,128)S(1)}, u32[]{:S(2)}, u32[]{:S(2)}) %collective-permute-start.3) | collective-permute-done | bytes 196640 | tf_op jit(solution)/shard_map/ppermute | solution.py:20
  62.1 5.6 %fusion.45 = f32[64,16,256]{2,1,0:T(8,128)S(1)} fusion(f32[64,16,256]{2,1,0:T(8,128)S(1)} %fusion.378, f32[64,3,256]{2,1,0:T(4,128)S(1)} %collective-permute-done.3, f32[64,3,256]{2,1,0:T(4,128)S(1)} %collective-permute-done.2, f32[]{:T(128)} %bitcast.45, f32[]{:T(128)} %bitcast.44, f32[]{:T(128)} %bitcast.43, f32[]{:T(128)} %bitcast.42, f32[]{:T(128)} %bitcast.41, ...), kind=kLoop, calls=%fused_computation.269 | loop fusion | flops 4980736 | bytes 2490396 | tf_op jit(solution)/shard_map/add | solution.py:33
  67.7 6.0 %fusion.321 = f32[64,16,256]{2,1,0:T(8,128)S(1)} fusion(f32[64,16,256]{2,1,0:T(8,128)S(1)} %fusion.45, f32[1,64,16,256]{3,2,1,0:T(8,128)S(1)} %copy-done.1, f32[]{:T(128)} %bitcast.51, f32[]{:T(128)} %bitcast.50, f32[]{:T(128)} %bitcast.49, f32[]{:T(128)} %bitcast.48, f32[]{:T(128)} %bitcast.47, f32[]{:T(128)} %bitcast.46, f32[]{:T(128)} %bitcast.7), kind=kLoop, calls=%fused_computation.545 | loop fusion | flops 3670016 | bytes 3145756 | tf_op jit(solution)/shard_map/div | solution.py:55
  73.7 4.3 %collective-permute-start.4 = (f32[15,16,256]{2,1,0:T(8,128)S(1)}, f32[15,16,256]{2,1,0:T(8,128)S(1)}, u32[]{:S(2)}, u32[]{:S(2)}) collective-permute-start(f32[15,16,256]{2,1,0:T(8,128)S(1)} %get-tuple-element.15), channel_id=1, source_target_pairs={{0,2},{2,4},{4,6},{6,8},{8,10},{10,12},{12,14},{1,3},{3,5},{5,7},{... | collective-permute-start | bytes 737288 | tf_op jit(solution)/shard_map/ppermute | solution.py:19
  78.0 1.3 collective-permute-start.5
  80.7 3.6 %collective-permute-done.4 = f32[15,16,256]{2,1,0:T(8,128)S(1)} collective-permute-done((f32[15,16,256]{2,1,0:T(8,128)S(1)}, f32[15,16,256]{2,1,0:T(8,128)S(1)}, u32[]{:S(2)}, u32[]{:S(2)}) %collective-permute-start.4) | collective-permute-done | bytes 245792 | tf_op jit(solution)/shard_map/ppermute | solution.py:19
  84.3 2.1 collective-permute-done.5
  86.4 23.6 %fusion.231 = f32[64,16,256]{2,1,0:T(8,128)S(1)} fusion(f32[64,16,256]{2,1,0:T(8,128)S(1)} %fusion.321, f32[15,16,256]{2,1,0:T(8,128)S(1)} %collective-permute-done.5, f32[15,16,256]{2,1,0:T(8,128)S(1)} %collective-permute-done.4, f32[]{:T(128)} %bitcast.81, f32[]{:T(128)} %bitcast.80, f32[]{:T(128)} %bitcast.79, f32[]{:T(128)} %bitcast.78, f32[]{:T(128)} %bitcast.77, ...), kind=kLoop, calls=%fused_computation.455 | loop fusion | flops 23855104 | bytes 2588796 | tf_op jit(solution)/shard_map/add | solution.py:33
  110.2 1.5 collective-permute-start.6
  111.6 1.3 collective-permute-start.7
  115.5 4.4 %collective-permute-done.7 = f32[64,3,256]{2,1,0:T(4,128)S(1)} collective-permute-done((f32[64,3,256]{2,1,0:T(4,128)S(1)}, f32[64,3,256]{2,1,0:T(4,128)S(1)}, u32[]{:S(2)}, u32[]{:S(2)}) %collective-permute-start.7) | collective-permute-done | bytes 196640 | tf_op jit(solution)/shard_map/ppermute | solution.py:20
  119.9 5.4 %fusion.31 = f32[64,16,256]{2,1,0:T(8,128)S(1)} fusion(f32[64,16,256]{2,1,0:T(8,128)S(1)} %fusion.231, f32[64,3,256]{2,1,0:T(4,128)S(1)} %collective-permute-done.7, f32[64,3,256]{2,1,0:T(4,128)S(1)} %collective-permute-done.6, f32[]{:T(128)} %bitcast.87, f32[]{:T(128)} %bitcast.86, f32[]{:T(128)} %bitcast.85, f32[]{:T(128)} %bitcast.84, f32[]{:T(128)} %bitcast.83, ...), kind=kLoop, calls=%fused_computation.255 | loop fusion | flops 4980736 | bytes 2490396 | tf_op jit(solution)/shard_map/add | solution.py:33
  125.3 7.0 %fusion.333 = f32[64,16,256]{2,1,0:T(8,128)} fusion(f32[64,16,256]{2,1,0:T(8,128)S(1)} %fusion.31, f32[]{:T(128)} %bitcast.93, f32[]{:T(128)} %bitcast.92, f32[]{:T(128)} %bitcast.91, f32[]{:T(128)} %bitcast.90, f32[]{:T(128)} %bitcast.89, f32[]{:T(128)} %bitcast.88, f32[]{:T(128)} %bitcast.1), kind=kLoop, calls=%fused_computation.557 | loop fusion | flops 3407872 | bytes 2097180 | tf_op jit(solution)/shard_map/add | solution.py:33
  132.6 14.5 %all-gather.5.cloned.1.call-done = f32[128,16,256]{2,1,0:T(8,128)} async-done(((f32[64,16,256]{2,1,0:T(8,128)}), f32[128,16,256]{2,1,0:T(8,128)}) %all-gather.5.cloned.1.call-update) | async-done | bytes 2097168 | tf_op jit(solution)/shard_map/all_gather | solution.py:57
  147.1 1.9 reduce_sum.48
  149.2 3.7 %collective-permute-start.8 = (f32[15,16,256]{2,1,0:T(8,128)S(1)}, f32[15,16,256]{2,1,0:T(8,128)S(1)}, u32[]{:S(2)}, u32[]{:S(2)}) collective-permute-start(f32[15,16,256]{2,1,0:T(8,128)S(1)} %get-tuple-element.11), channel_id=1, source_target_pairs={{0,2},{2,4},{4,6},{6,8},{8,10},{10,12},{12,14},{1,3},{3,5},{5,7},{... | collective-permute-start | bytes 737288 | tf_op jit(solution)/shard_map/ppermute | solution.py:19
  152.9 1.3 collective-permute-start.9
  154.2 9.6 %collective-permute-done.8 = f32[15,16,256]{2,1,0:T(8,128)S(1)} collective-permute-done((f32[15,16,256]{2,1,0:T(8,128)S(1)}, f32[15,16,256]{2,1,0:T(8,128)S(1)}, u32[]{:S(2)}, u32[]{:S(2)}) %collective-permute-start.8) | collective-permute-done | bytes 245792 | tf_op jit(solution)/shard_map/ppermute | solution.py:19
  163.8 23.7 %fusion.145 = f32[64,16,256]{2,1,0:T(8,128)S(1)} fusion(f32[64,16,256]{2,1,0:T(8,128)S(1)} %multiply_multiply_fusion.1, f32[15,16,256]{2,1,0:T(8,128)S(1)} %collective-permute-done.9, f32[15,16,256]{2,1,0:T(8,128)S(1)} %collective-permute-done.8, f32[]{:T(128)} %bitcast.39, f32[]{:T(128)} %bitcast.38, f32[]{:T(128)} %bitcast.37, f32[]{:T(128)} %bitcast.36, ...), kind=kLoop, calls=%fused_computation.369 | loop fusion | flops 23855104 | bytes 2588796 | tf_op jit(solution)/shard_map/add | solution.py:33
  187.6 3.4 %collective-permute-start.10 = (f32[64,3,256]{2,1,0:T(4,128)S(1)}, f32[64,3,256]{2,1,0:T(4,128)S(1)}, u32[]{:S(2)}, u32[]{:S(2)}) collective-permute-start(f32[64,3,256]{2,1,0:T(4,128)S(1)} %get-tuple-element.9), channel_id=1, source_target_pairs={{0,1},{2,3},{4,5},{6,7},{8,9},{10,11},{12,13},{14,15},{16,17},{18,... | collective-permute-start | bytes 589832 | tf_op jit(solution)/shard_map/ppermute | solution.py:19
  191.0 1.4 collective-permute-start.11
  192.4 3.5 %collective-permute-done.10 = f32[64,3,256]{2,1,0:T(4,128)S(1)} collective-permute-done((f32[64,3,256]{2,1,0:T(4,128)S(1)}, f32[64,3,256]{2,1,0:T(4,128)S(1)}, u32[]{:S(2)}, u32[]{:S(2)}) %collective-permute-start.10) | collective-permute-done | bytes 196640 | tf_op jit(solution)/shard_map/ppermute | solution.py:19
  196.0 4.3 %collective-permute-done.11 = f32[64,3,256]{2,1,0:T(4,128)S(1)} collective-permute-done((f32[64,3,256]{2,1,0:T(4,128)S(1)}, f32[64,3,256]{2,1,0:T(4,128)S(1)}, u32[]{:S(2)}, u32[]{:S(2)}) %collective-permute-start.11) | collective-permute-done | bytes 196640 | tf_op jit(solution)/shard_map/ppermute | solution.py:20
  200.3 5.5 %fusion.17 = f32[64,16,256]{2,1,0:T(8,128)S(1)} fusion(f32[64,16,256]{2,1,0:T(8,128)S(1)} %fusion.145, f32[64,3,256]{2,1,0:T(4,128)S(1)} %collective-permute-done.11, f32[64,3,256]{2,1,0:T(4,128)S(1)} %collective-permute-done.10, f32[]{:T(128)} %bitcast.45, f32[]{:T(128)} %bitcast.44, f32[]{:T(128)} %bitcast.43, f32[]{:T(128)} %bitcast.42, f32[]{:T(128)} %bitcast.41, ...), kind=kLoop, calls=%fused_computation.241 | loop fusion | flops 4980736 | bytes 2490396 | tf_op jit(solution)/shard_map/add | solution.py:33
  205.8 6.0 %fusion.346 = f32[64,16,256]{2,1,0:T(8,128)S(1)} fusion(f32[64,16,256]{2,1,0:T(8,128)S(1)} %fusion.17, f32[1,64,16,256]{3,2,1,0:T(8,128)S(1)} %copy-done.2, f32[]{:T(128)} %bitcast.51, f32[]{:T(128)} %bitcast.50, f32[]{:T(128)} %bitcast.49, f32[]{:T(128)} %bitcast.48, f32[]{:T(128)} %bitcast.47, f32[]{:T(128)} %bitcast.46, f32[]{:T(128)} %bitcast.7), kind=kLoop, calls=%fused_computation.570 | loop fusion | flops 3670016 | bytes 3145756 | tf_op jit(solution)/shard_map/div | solution.py:55
  211.8 4.5 %collective-permute-start.12 = (f32[15,16,256]{2,1,0:T(8,128)S(1)}, f32[15,16,256]{2,1,0:T(8,128)S(1)}, u32[]{:S(2)}, u32[]{:S(2)}) collective-permute-start(f32[15,16,256]{2,1,0:T(8,128)S(1)} %get-tuple-element.7), channel_id=1, source_target_pairs={{0,2},{2,4},{4,6},{6,8},{8,10},{10,12},{12,14},{1,3},{3,5},{5,7},{... | collective-permute-start | bytes 737288 | tf_op jit(solution)/shard_map/ppermute | solution.py:19
  216.3 1.3 collective-permute-start.13
  217.6 2.4 collective-permute-done.12
  220.0 5.9 %collective-permute-done.13 = f32[15,16,256]{2,1,0:T(8,128)S(1)} collective-permute-done((f32[15,16,256]{2,1,0:T(8,128)S(1)}, f32[15,16,256]{2,1,0:T(8,128)S(1)}, u32[]{:S(2)}, u32[]{:S(2)}) %collective-permute-start.13) | collective-permute-done | bytes 245792 | tf_op jit(solution)/shard_map/ppermute | solution.py:20
  225.9 23.6 %fusion.59 = f32[64,16,256]{2,1,0:T(8,128)S(1)} fusion(f32[64,16,256]{2,1,0:T(8,128)S(1)} %fusion.346, f32[15,16,256]{2,1,0:T(8,128)S(1)} %collective-permute-done.13, f32[15,16,256]{2,1,0:T(8,128)S(1)} %collective-permute-done.12, f32[]{:T(128)} %bitcast.81, f32[]{:T(128)} %bitcast.80, f32[]{:T(128)} %bitcast.79, f32[]{:T(128)} %bitcast.78, f32[]{:T(128)} %bitcast.77, ...), kind=kLoop, calls=%fused_computation.283 | loop fusion | flops 23855104 | bytes 2588796 | tf_op jit(solution)/shard_map/add | solution.py:33
  249.6 1.5 collective-permute-start.14
  251.1 1.3 collective-permute-start.15
  252.4 2.6 collective-permute-done.14
  254.9 4.4 %collective-permute-done.15 = f32[64,3,256]{2,1,0:T(4,128)S(1)} collective-permute-done((f32[64,3,256]{2,1,0:T(4,128)S(1)}, f32[64,3,256]{2,1,0:T(4,128)S(1)}, u32[]{:S(2)}, u32[]{:S(2)}) %collective-permute-start.15) | collective-permute-done | bytes 196640 | tf_op jit(solution)/shard_map/ppermute | solution.py:20
  259.4 5.4 %fusion.3 = f32[64,16,256]{2,1,0:T(8,128)S(1)} fusion(f32[64,16,256]{2,1,0:T(8,128)S(1)} %fusion.59, f32[64,3,256]{2,1,0:T(4,128)S(1)} %collective-permute-done.15, f32[64,3,256]{2,1,0:T(4,128)S(1)} %collective-permute-done.14, f32[]{:T(128)} %bitcast.87, f32[]{:T(128)} %bitcast.86, f32[]{:T(128)} %bitcast.85, f32[]{:T(128)} %bitcast.84, f32[]{:T(128)} %bitcast.83, ...), kind=kLoop, calls=%fused_computation.227 | loop fusion | flops 4980736 | bytes 2490396 | tf_op jit(solution)/shard_map/add | solution.py:33
  264.8 7.0 %fusion.358 = f32[64,16,256]{2,1,0:T(8,128)} fusion(f32[64,16,256]{2,1,0:T(8,128)S(1)} %fusion.3, f32[]{:T(128)} %bitcast.93, f32[]{:T(128)} %bitcast.92, f32[]{:T(128)} %bitcast.91, f32[]{:T(128)} %bitcast.90, f32[]{:T(128)} %bitcast.89, f32[]{:T(128)} %bitcast.88, f32[]{:T(128)} %bitcast.1), kind=kLoop, calls=%fused_computation.582 | loop fusion | flops 3407872 | bytes 2097180 | tf_op jit(solution)/shard_map/add | solution.py:33
  271.8 14.8 %all-gather.7.cloned.1.call-done = f32[128,16,256]{2,1,0:T(8,128)} async-done(((f32[64,16,256]{2,1,0:T(8,128)}), f32[128,16,256]{2,1,0:T(8,128)}) %all-gather.7.cloned.1.call-update) | async-done | bytes 2097168 | tf_op jit(solution)/shard_map/all_gather | solution.py:57
  286.6 1.9 reduce_sum.49
  (40 shorter events, 15.2 us)
Async XLA Ops:
  6.5 18.8 %copy-start = (f32[64,16,256]{2,1,0:T(8,128)S(1)}, f32[64,16,256]{2,1,0:T(8,128)}, u32[]{:S(2)}) copy-start(f32[64,16,256]{2,1,0:T(8,128)} %param.6) | copy-start | bytes 3145732
  6.5 140.5 %all-gather.5.cloned.1.call-start = ((), (), s32[]{:S(2)}) async-start(), calls=%async_computation | async-start | bytes 3145728 | tf_op jit(solution)/shard_map/all_gather | solution.py:57
  7.7 17.6 %collective-permute-start = (f32[15,16,256]{2,1,0:T(8,128)S(1)}, f32[15,16,256]{2,1,0:T(8,128)S(1)}, u32[]{:S(2)}, u32[]{:S(2)}) collective-permute-start(f32[15,16,256]{2,1,0:T(8,128)S(1)} %get-tuple-element.21), channel_id=1, source_target_pairs={{0,2},{2,4},{4,6},{6,8},{8,10},{10,12},{12,14},{1,3},{3,5},{5,7},{... | collective-permute-start | bytes 737288 | tf_op jit(solution)/shard_map/ppermute | solution.py:19
  12.6 13.0 %collective-permute-start.1 = (f32[15,16,256]{2,1,0:T(8,128)S(1)}, f32[15,16,256]{2,1,0:T(8,128)S(1)}, u32[]{:S(2)}, u32[]{:S(2)}) collective-permute-start(f32[15,16,256]{2,1,0:T(8,128)S(1)} %get-tuple-element.22), channel_id=1, source_target_pairs={{2,0},{4,2},{6,4},{8,6},{10,8},{12,10},{14,12},{3,1},{5,3},{7,5},{... | collective-permute-start | bytes 737288 | tf_op jit(solution)/shard_map/ppermute | solution.py:20
  49.3 8.7 %collective-permute-start.2 = (f32[64,3,256]{2,1,0:T(4,128)S(1)}, f32[64,3,256]{2,1,0:T(4,128)S(1)}, u32[]{:S(2)}, u32[]{:S(2)}) collective-permute-start(f32[64,3,256]{2,1,0:T(4,128)S(1)} %get-tuple-element.17), channel_id=1, source_target_pairs={{0,1},{2,3},{4,5},{6,7},{8,9},{10,11},{12,13},{14,15},{16,17},{18,... | collective-permute-start | bytes 589832 | tf_op jit(solution)/shard_map/ppermute | solution.py:19
  52.7 9.4 %collective-permute-start.3 = (f32[64,3,256]{2,1,0:T(4,128)S(1)}, f32[64,3,256]{2,1,0:T(4,128)S(1)}, u32[]{:S(2)}, u32[]{:S(2)}) collective-permute-start(f32[64,3,256]{2,1,0:T(4,128)S(1)} %get-tuple-element.18), channel_id=1, source_target_pairs={{1,0},{3,2},{5,4},{7,6},{9,8},{11,10},{13,12},{15,14},{17,16},{19,... | collective-permute-start | bytes 589832 | tf_op jit(solution)/shard_map/ppermute | solution.py:20
  62.1 5.6 %copy-start.1 = (f32[1,64,16,256]{3,2,1,0:T(8,128)S(1)}, f32[1,64,16,256]{3,2,1,0:T(8,128)}, u32[]{:S(2)}) copy-start(f32[1,64,16,256]{3,2,1,0:T(8,128)} %param.5) | copy-start | bytes 3145732
  73.7 10.6 %collective-permute-start.4 = (f32[15,16,256]{2,1,0:T(8,128)S(1)}, f32[15,16,256]{2,1,0:T(8,128)S(1)}, u32[]{:S(2)}, u32[]{:S(2)}) collective-permute-start(f32[15,16,256]{2,1,0:T(8,128)S(1)} %get-tuple-element.15), channel_id=1, source_target_pairs={{0,2},{2,4},{4,6},{6,8},{8,10},{10,12},{12,14},{1,3},{3,5},{5,7},{... | collective-permute-start | bytes 737288 | tf_op jit(solution)/shard_map/ppermute | solution.py:19
  78.0 8.5 %collective-permute-start.5 = (f32[15,16,256]{2,1,0:T(8,128)S(1)}, f32[15,16,256]{2,1,0:T(8,128)S(1)}, u32[]{:S(2)}, u32[]{:S(2)}) collective-permute-start(f32[15,16,256]{2,1,0:T(8,128)S(1)} %get-tuple-element.16), channel_id=1, source_target_pairs={{2,0},{4,2},{6,4},{8,6},{10,8},{12,10},{14,12},{3,1},{5,3},{7,5},{... | collective-permute-start | bytes 737288 | tf_op jit(solution)/shard_map/ppermute | solution.py:20
  110.2 5.3 %collective-permute-start.6 = (f32[64,3,256]{2,1,0:T(4,128)S(1)}, f32[64,3,256]{2,1,0:T(4,128)S(1)}, u32[]{:S(2)}, u32[]{:S(2)}) collective-permute-start(f32[64,3,256]{2,1,0:T(4,128)S(1)} %get-tuple-element.13), channel_id=1, source_target_pairs={{0,1},{2,3},{4,5},{6,7},{8,9},{10,11},{12,13},{14,15},{16,17},{18,... | collective-permute-start | bytes 589832 | tf_op jit(solution)/shard_map/ppermute | solution.py:19
  111.6 8.3 %collective-permute-start.7 = (f32[64,3,256]{2,1,0:T(4,128)S(1)}, f32[64,3,256]{2,1,0:T(4,128)S(1)}, u32[]{:S(2)}, u32[]{:S(2)}) collective-permute-start(f32[64,3,256]{2,1,0:T(4,128)S(1)} %get-tuple-element.14), channel_id=1, source_target_pairs={{1,0},{3,2},{5,4},{7,6},{9,8},{11,10},{13,12},{15,14},{17,16},{19,... | collective-permute-start | bytes 589832 | tf_op jit(solution)/shard_map/ppermute | solution.py:20
  132.3 154.3 %all-gather.7.cloned.1.call-start = ((), (), s32[]{:S(2)}) async-start(), calls=%async_computation.1 | async-start | bytes 3145728 | tf_op jit(solution)/shard_map/all_gather | solution.py:57
  149.2 14.6 %collective-permute-start.8 = (f32[15,16,256]{2,1,0:T(8,128)S(1)}, f32[15,16,256]{2,1,0:T(8,128)S(1)}, u32[]{:S(2)}, u32[]{:S(2)}) collective-permute-start(f32[15,16,256]{2,1,0:T(8,128)S(1)} %get-tuple-element.11), channel_id=1, source_target_pairs={{0,2},{2,4},{4,6},{6,8},{8,10},{10,12},{12,14},{1,3},{3,5},{5,7},{... | collective-permute-start | bytes 737288 | tf_op jit(solution)/shard_map/ppermute | solution.py:19
  152.9 10.9 %collective-permute-start.9 = (f32[15,16,256]{2,1,0:T(8,128)S(1)}, f32[15,16,256]{2,1,0:T(8,128)S(1)}, u32[]{:S(2)}, u32[]{:S(2)}) collective-permute-start(f32[15,16,256]{2,1,0:T(8,128)S(1)} %get-tuple-element.12), channel_id=1, source_target_pairs={{2,0},{4,2},{6,4},{8,6},{10,8},{12,10},{14,12},{3,1},{5,3},{7,5},{... | collective-permute-start | bytes 737288 | tf_op jit(solution)/shard_map/ppermute | solution.py:20
  187.6 8.4 %collective-permute-start.10 = (f32[64,3,256]{2,1,0:T(4,128)S(1)}, f32[64,3,256]{2,1,0:T(4,128)S(1)}, u32[]{:S(2)}, u32[]{:S(2)}) collective-permute-start(f32[64,3,256]{2,1,0:T(4,128)S(1)} %get-tuple-element.9), channel_id=1, source_target_pairs={{0,1},{2,3},{4,5},{6,7},{8,9},{10,11},{12,13},{14,15},{16,17},{18,... | collective-permute-start | bytes 589832 | tf_op jit(solution)/shard_map/ppermute | solution.py:19
  191.0 14.8 %copy-start.2 = (f32[1,64,16,256]{3,2,1,0:T(8,128)S(1)}, f32[1,64,16,256]{3,2,1,0:T(8,128)}, u32[]{:S(2)}) copy-start(f32[1,64,16,256]{3,2,1,0:T(8,128)} %param.5) | copy-start | bytes 3145732
  191.0 9.2 %collective-permute-start.11 = (f32[64,3,256]{2,1,0:T(4,128)S(1)}, f32[64,3,256]{2,1,0:T(4,128)S(1)}, u32[]{:S(2)}, u32[]{:S(2)}) collective-permute-start(f32[64,3,256]{2,1,0:T(4,128)S(1)} %get-tuple-element.10), channel_id=1, source_target_pairs={{1,0},{3,2},{5,4},{7,6},{9,8},{11,10},{13,12},{15,14},{17,16},{19,... | collective-permute-start | bytes 589832 | tf_op jit(solution)/shard_map/ppermute | solution.py:20
  211.8 8.2 %collective-permute-start.12 = (f32[15,16,256]{2,1,0:T(8,128)S(1)}, f32[15,16,256]{2,1,0:T(8,128)S(1)}, u32[]{:S(2)}, u32[]{:S(2)}) collective-permute-start(f32[15,16,256]{2,1,0:T(8,128)S(1)} %get-tuple-element.7), channel_id=1, source_target_pairs={{0,2},{2,4},{4,6},{6,8},{8,10},{10,12},{12,14},{1,3},{3,5},{5,7},{... | collective-permute-start | bytes 737288 | tf_op jit(solution)/shard_map/ppermute | solution.py:19
  216.3 9.6 %collective-permute-start.13 = (f32[15,16,256]{2,1,0:T(8,128)S(1)}, f32[15,16,256]{2,1,0:T(8,128)S(1)}, u32[]{:S(2)}, u32[]{:S(2)}) collective-permute-start(f32[15,16,256]{2,1,0:T(8,128)S(1)} %get-tuple-element.8), channel_id=1, source_target_pairs={{2,0},{4,2},{6,4},{8,6},{10,8},{12,10},{14,12},{3,1},{5,3},{7,5},{... | collective-permute-start | bytes 737288 | tf_op jit(solution)/shard_map/ppermute | solution.py:20
  249.6 5.3 %collective-permute-start.14 = (f32[64,3,256]{2,1,0:T(4,128)S(1)}, f32[64,3,256]{2,1,0:T(4,128)S(1)}, u32[]{:S(2)}, u32[]{:S(2)}) collective-permute-start(f32[64,3,256]{2,1,0:T(4,128)S(1)} %get-tuple-element.5), channel_id=1, source_target_pairs={{0,1},{2,3},{4,5},{6,7},{8,9},{10,11},{12,13},{14,15},{16,17},{18,... | collective-permute-start | bytes 589832 | tf_op jit(solution)/shard_map/ppermute | solution.py:19
  251.1 8.3 %collective-permute-start.15 = (f32[64,3,256]{2,1,0:T(4,128)S(1)}, f32[64,3,256]{2,1,0:T(4,128)S(1)}, u32[]{:S(2)}, u32[]{:S(2)}) collective-permute-start(f32[64,3,256]{2,1,0:T(4,128)S(1)} %get-tuple-element.6), channel_id=1, source_target_pairs={{1,0},{3,2},{5,4},{7,6},{9,8},{11,10},{13,12},{15,14},{17,16},{19,... | collective-permute-start | bytes 589832 | tf_op jit(solution)/shard_map/ppermute | solution.py:20
Sparse Core Ops, SparseCore 0:
  132.5 14.5 all-gather.4
  271.9 14.6 all-gather.6
